TPU v7x, 256 devices: a whole 4x4x8 slice. The times are simulated.
256 devices in a mesh: dp: 8 (over y, x_hi), ctx: 32 (over x_lo, z, core).
Axes of the slice: x: 4 (x_hi: 2, x_lo: 2; x = x_hi * 2 + x_lo), y: 4, z: 8, core: 2. Of those that a mesh axis runs over, the one named last changes fastest.
Arguments:
- inputs: bfloat16 [8, 32, 128, 4096], P('dp', 'ctx'), may hold values from -6 to 6
- queries: bfloat16 [8, 32, 128, 1024], P('dp', 'ctx'), may hold values from -6 to 6
- keys_values: bfloat16 [8, 32, 128, 256], P('dp', 'ctx'), may hold values from -6 to 6
- out_grad: bfloat16 [8, 32, 128, 1024], P('dp', 'ctx'), may hold values from -6 to 6
- lengths: int32 [8, 10], P('dp'), may hold values from 1 to 1024, 4096 in all within a row
Outputs:
- grad_q: bfloat16 [8, 32, 128, 1024], P('dp', 'ctx')
- grad_kv: bfloat16 [8, 32, 128, 256], P('dp', 'ctx')
- grad_kv_weight: float32 [4096, 256], P('ctx')
All inputs are finite; a program needn't handle non-finite values.
Results may differ from a plain program's by a relative error of at most 0.0052.
Values may be sent and summed in bfloat16 or wider, within the bound.
A program may use at most 64 MiB of HBM per device.

v0:
```python
import jax
import jax.numpy as jnp
from jax import lax
from jax.sharding import PartitionSpec as P

HD = 128
RESPONSES = 4
neg_fill = -1e30


def from_behind(x, axis, by):
    length = lax.axis_size(axis)
    return lax.ppermute(x, axis, [(i, (i + by) % length) for i in range(length)])


def piece_of(positions, piece_ends):
    return jnp.sum((positions[:, None] >= piece_ends[None, :]).astype(jnp.int32), axis=1)


def allowed_pairs(query_pos, key_pos, piece_ends):
    per_group = RESPONSES + 1
    query_piece = piece_of(query_pos, piece_ends)
    key_piece = piece_of(key_pos, piece_ends)
    same_group = (query_piece // per_group)[:, None] == (key_piece // per_group)[None, :]
    visible = (key_piece % per_group == 0)[None, :] | (query_piece[:, None] == key_piece[None, :])
    return (key_pos[None, :] <= query_pos[:, None]) & same_group & visible


def contract_rows(left_side, right_side):
    return lax.dot_general(
        left_side, right_side, (((0,), (0,)), ((), ())), preferred_element_type=jnp.float32
    )


def on_device(inputs, queries, keys_values, out_grad, lengths):
    stripe_count = lax.axis_size("ctx")
    my_stripe = lax.axis_index("ctx")
    local_count = queries.shape[2]
    q_width = queries.shape[3]
    head_count = q_width // HD
    row_total = local_count * head_count
    score_scale = HD ** (-0.5)
    x_local = inputs[0, 0]
    q_rows = queries[0, 0].reshape(row_total, HD)
    grad_rows = out_grad[0, 0].reshape(row_total, HD)
    kv_local = keys_values[0, 0]
    piece_ends = jnp.cumsum(lengths[0], dtype=jnp.int32)
    query_pos = jnp.arange(local_count, dtype=jnp.int32) * stripe_count + my_stripe

    def row_mask(key_pos):
        key_count = key_pos.shape[0]
        allowed = allowed_pairs(query_pos, key_pos, piece_ends)
        return jnp.broadcast_to(allowed[:, None, :], (local_count, head_count, key_count)).reshape(
            row_total, key_count
        )

    def gathered_pos(first_row, row_count):
        key_rows = first_row + jnp.arange(row_count, dtype=jnp.int32)
        return key_rows % local_count * stripe_count + key_rows // local_count

    def forward_block(carried, kv_block, key_pos):
        running_max, running_sum, weighted = carried
        allowed = row_mask(key_pos)
        scores = (
            jnp.dot(q_rows, kv_block[:, :HD].T, preferred_element_type=jnp.float32) * score_scale
        )
        prob_grad = jnp.dot(grad_rows, kv_block[:, HD:].T, preferred_element_type=jnp.float32)
        new_max = jnp.maximum(running_max, jnp.max(jnp.where(allowed, scores, neg_fill), axis=1))
        factor = jnp.exp(running_max - new_max)
        expo_terms = jnp.where(allowed, jnp.exp(scores - new_max[:, None]), 0.0)
        new_sum = running_sum * factor + jnp.sum(expo_terms, axis=1)
        new_weighted = weighted * factor + jnp.sum(expo_terms * prob_grad, axis=1)
        return (new_max, new_sum, new_weighted)

    init_state = (
        jnp.full((row_total,), neg_fill, jnp.float32),
        jnp.zeros((row_total,), jnp.float32),
        jnp.zeros((row_total,), jnp.float32),
    )
    carried = init_state
    kv_piece = lax.all_gather(kv_local, "ctx", axis=0, tiled=True)
    row_count = kv_piece.shape[0]
    sub_blocks = kv_piece.reshape(row_count // 512, 512, kv_piece.shape[1])

    def inner_step(state_now, sub_item):
        sub_block, sub_index = sub_item
        return (forward_block(state_now, sub_block, gathered_pos(sub_index * 512, 512)), None)

    carried, unused = lax.scan(
        inner_step, carried, (sub_blocks, jnp.arange(row_count // 512, dtype=jnp.int32))
    )
    running_max, running_sum, weighted = carried
    log_total = running_max + jnp.log(running_sum)
    row_delta = weighted / running_sum

    def backward_block(grad_q, kv_block, key_pos):
        allowed = row_mask(key_pos)
        scores = (
            jnp.dot(q_rows, kv_block[:, :HD].T, preferred_element_type=jnp.float32) * score_scale
        )
        soft_probs = jnp.where(allowed, jnp.exp(scores - log_total[:, None]), 0.0)
        prob_grad = jnp.dot(grad_rows, kv_block[:, HD:].T, preferred_element_type=jnp.float32)
        score_grad = soft_probs * (prob_grad - row_delta[:, None])
        low_probs = soft_probs.astype(jnp.bfloat16)
        low_score = score_grad.astype(jnp.bfloat16)
        grad_q = (
            grad_q
            + jnp.dot(low_score, kv_block[:, :HD], preferred_element_type=jnp.float32) * score_scale
        )
        key_term = contract_rows(low_score, q_rows) * score_scale
        value_term = contract_rows(low_probs, grad_rows)
        return (grad_q, jnp.concatenate([key_term, value_term], axis=1))

    zero_grad = jnp.zeros((row_total, HD), jnp.float32)

    def cycle_step(cycle_index, state_now):
        grad_q, kv_block, key_grads = state_now
        source = (my_stripe - cycle_index) % stripe_count
        key_pos = jnp.arange(local_count, dtype=jnp.int32) * stripe_count + source
        grad_q, key_term = backward_block(grad_q, kv_block, key_pos)
        kv_block = from_behind(kv_block, "ctx", 1)
        key_grads = from_behind(key_grads + key_term, "ctx", 1)
        return (grad_q, kv_block, key_grads)

    def cycle_pair(pair_index, state_now):
        return cycle_step(2 * pair_index + 1, cycle_step(2 * pair_index, state_now))

    start_state = (zero_grad, kv_local, jnp.zeros((local_count, 2 * HD), jnp.float32))
    grad_q, spent_kv, key_grads = lax.fori_loop(0, stripe_count // 2, cycle_pair, start_state)
    kv_grad_low = key_grads.astype(jnp.bfloat16)
    grad_q_out = grad_q.astype(jnp.bfloat16).reshape(1, 1, local_count, q_width)
    dp_count = lax.axis_size("dp")
    weight_shard = lax.psum_scatter(
        contract_rows(x_local, kv_grad_low), "ctx", scatter_dimension=0, tiled=True
    )
    weight_total = lax.psum(weight_shard, "dp")
    return (grad_q_out, kv_grad_low.reshape(1, 1, local_count, 2 * HD), weight_total / dp_count)


def solution(mesh):
    return jax.shard_map(
        on_device,
        mesh=mesh,
        in_specs=(
            P("dp", "ctx", None, None),
            P("dp", "ctx", None, None),
            P("dp", "ctx", None, None),
            P("dp", "ctx", None, None),
            P("dp", None),
        ),
        out_specs=(P("dp", "ctx", None, None), P("dp", "ctx", None, None), P("ctx", None)),
        check_vma=False,
    )
```

profile of v0, /device:TPU:32, one launch (start us, length us, event | category | flops | bytes accessed | tf_op | source)
XLA Modules:
  0.0 600.0 jit_solution(14512297040010059716)
XLA Ops:
  12.6 64.4 %all-gather.3.cloned.1.call-done = bf16[1,1,4096,256]{3,2,1,0:T(8,128)(2,1)} async-done(((bf16[1,1,128,256]{3,2,1,0:T(8,128)(2,1)}), bf16[1,1,4096,256]{3,2,1,0:T(8,128)(2,1)}) %all-gather.3.cloned.1.call-update) | async-done | bytes 2097168 | tf_op jit(solution)/shard_map/all_gather | solution.py:81
  77.0 55.5 %while.41 = (s32[]{:T(128)}, f32[1024]{0:T(1024)S(1)}, f32[1024]{0:T(1024)S(1)}, f32[1024]{0:T(1024)S(1)}, s32[8]{0:T(128)S(1)}, /*index=5*/s32[10]{0:T(128)S(1)...) while((s32[]{:T(128)}, f32[1024]{0:T(1024)S(1)}, ...), condition=%wide.region_7.8_spmd.clone, body=%wide.region_1.7_spmd.clone.sunk | while | flops 275166080 | bytes 18316680 | solution.py:89
  132.5 242.1 %while.42 = (s32[]{:T(128)}, f32[1024,128]{1,0:T(8,128)}, bf16[128,256]{1,0:T(8,128)(2,1)S(1)}, f32[128,256]{0,1:T(8,128)S(1)}, s32[]{:T(128)}, /*index=5*/s32[1...) while((s32[]{:T(128)}, f32[1024,128]{1,0:T(8,128)}, ...), condition=%wide.region_12.13_spmd.clone.clone.clone, body=%wide.region_8.12_spmd.clone.clone.clone.sunk | while | flops 338411936 | bytes 14973101 | solution.py:129
  166.1 3.0 collective-permute-done.1
  174.3 3.0 collective-permute-done
  181.7 3.0 collective-permute-done.1
  189.9 3.0 collective-permute-done
  197.3 3.0 collective-permute-done.1
  205.6 3.0 collective-permute-done
  212.9 3.0 collective-permute-done.1
  221.2 3.0 collective-permute-done
  236.8 3.0 collective-permute-done
  252.4 3.0 collective-permute-done
  268.0 3.0 collective-permute-done
  275.4 3.0 collective-permute-done.1
  283.7 3.0 collective-permute-done
  299.3 3.0 collective-permute-done
  314.9 3.0 collective-permute-done
  322.3 3.0 collective-permute-done.1
  330.5 3.0 collective-permute-done
  346.1 3.0 collective-permute-done
  361.8 3.0 collective-permute-done
  377.5 123.0 %reduce-scatter.2.cloned.1.call-done = f32[128,256]{0,1:T(8,128)} async-done(((f32[4096,256]{0,1:T(8,128)}), f32[128,256]{0,1:T(8,128)}) %reduce-scatter.2.cloned.1.call-update) | async-done | bytes 131088 | tf_op jit(solution)/shard_map/reduce_scatter | solution.py:133
  501.4 90.5 %all-reduce.2.cloned.1.call-done = f32[128,256]{0,1:T(8,128)} async-done(((f32[128,256]{0,1:T(8,128)}), f32[128,256]{0,1:T(8,128)}) %all-reduce.2.cloned.1.call-update) | async-done | bytes 131088 | tf_op jit(solution)/shard_map/psum | solution.py:136
  (748 shorter events, 242.3 us)
Async XLA Ops:
  7.2 69.8 %all-gather.3.cloned.1.call-start = ((), (), s32[]{:S(2)}) async-start(), calls=%async_computation.3 | async-start | bytes 2162688 | tf_op jit(solution)/shard_map/all_gather | solution.py:81
  8.8 491.7 %reduce-scatter.2.cloned.1.call-start = ((), (), s32[]{:S(2)}) async-start(), calls=%async_computation.1 | async-start | bytes 4325376 | tf_op jit(solution)/shard_map/reduce_scatter | solution.py:133
  165.0 6.6 %collective-permute-start.3 = (f32[128,256]{0,1:T(8,128)S(1)}, f32[128,256]{0,1:T(8,128)S(1)}, u32[]{:S(2)}, u32[]{:S(2)}) collective-permute-start(f32[128,256]{0,1:T(8,128)S(1)} %maximum_add_fusion.5), channel_id=1, source_target_pairs={{0,1},{1,2},{2,3},{3,4},{4,5},{5,6},{6,7},{7,8},{8,9},{9,10},{10,1... | collective-permute-start | bytes 393224 | tf_op jit(solution)/shard_map/while/body/eval_jaxpr/ppermute | solution.py:13
  174.0 6.6 %collective-permute-start.2 = (f32[128,256]{0,1:T(8,128)S(1)}, f32[128,256]{0,1:T(8,128)S(1)}, u32[]{:S(2)}, u32[]{:S(2)}) collective-permute-start(f32[128,256]{0,1:T(8,128)S(1)} %maximum_add_fusion.4), channel_id=1, source_target_pairs={{0,1},{1,2},{2,3},{3,4},{4,5},{5,6},{6,7},{7,8},{8,9},{9,10},{10,1... | collective-permute-start | bytes 393224 | tf_op jit(solution)/shard_map/while/body/eval_jaxpr/ppermute | solution.py:13
  180.6 6.6 %collective-permute-start.3 = (f32[128,256]{0,1:T(8,128)S(1)}, f32[128,256]{0,1:T(8,128)S(1)}, u32[]{:S(2)}, u32[]{:S(2)}) collective-permute-start(f32[128,256]{0,1:T(8,128)S(1)} %maximum_add_fusion.5), channel_id=1, source_target_pairs={{0,1},{1,2},{2,3},{3,4},{4,5},{5,6},{6,7},{7,8},{8,9},{9,10},{10,1... | collective-permute-start | bytes 393224 | tf_op jit(solution)/shard_map/while/body/eval_jaxpr/ppermute | solution.py:13
  189.6 6.6 %collective-permute-start.2 = (f32[128,256]{0,1:T(8,128)S(1)}, f32[128,256]{0,1:T(8,128)S(1)}, u32[]{:S(2)}, u32[]{:S(2)}) collective-permute-start(f32[128,256]{0,1:T(8,128)S(1)} %maximum_add_fusion.4), channel_id=1, source_target_pairs={{0,1},{1,2},{2,3},{3,4},{4,5},{5,6},{6,7},{7,8},{8,9},{9,10},{10,1... | collective-permute-start | bytes 393224 | tf_op jit(solution)/shard_map/while/body/eval_jaxpr/ppermute | solution.py:13
  196.2 6.6 %collective-permute-start.3 = (f32[128,256]{0,1:T(8,128)S(1)}, f32[128,256]{0,1:T(8,128)S(1)}, u32[]{:S(2)}, u32[]{:S(2)}) collective-permute-start(f32[128,256]{0,1:T(8,128)S(1)} %maximum_add_fusion.5), channel_id=1, source_target_pairs={{0,1},{1,2},{2,3},{3,4},{4,5},{5,6},{6,7},{7,8},{8,9},{9,10},{10,1... | collective-permute-start | bytes 393224 | tf_op jit(solution)/shard_map/while/body/eval_jaxpr/ppermute | solution.py:13
  211.8 6.6 %collective-permute-start.3 = (f32[128,256]{0,1:T(8,128)S(1)}, f32[128,256]{0,1:T(8,128)S(1)}, u32[]{:S(2)}, u32[]{:S(2)}) collective-permute-start(f32[128,256]{0,1:T(8,128)S(1)} %maximum_add_fusion.5), channel_id=1, source_target_pairs={{0,1},{1,2},{2,3},{3,4},{4,5},{5,6},{6,7},{7,8},{8,9},{9,10},{10,1... | collective-permute-start | bytes 393224 | tf_op jit(solution)/shard_map/while/body/eval_jaxpr/ppermute | solution.py:13
  220.9 6.6 %collective-permute-start.2 = (f32[128,256]{0,1:T(8,128)S(1)}, f32[128,256]{0,1:T(8,128)S(1)}, u32[]{:S(2)}, u32[]{:S(2)}) collective-permute-start(f32[128,256]{0,1:T(8,128)S(1)} %maximum_add_fusion.4), channel_id=1, source_target_pairs={{0,1},{1,2},{2,3},{3,4},{4,5},{5,6},{6,7},{7,8},{8,9},{9,10},{10,1... | collective-permute-start | bytes 393224 | tf_op jit(solution)/shard_map/while/body/eval_jaxpr/ppermute | solution.py:13
  227.4 6.6 %collective-permute-start.3 = (f32[128,256]{0,1:T(8,128)S(1)}, f32[128,256]{0,1:T(8,128)S(1)}, u32[]{:S(2)}, u32[]{:S(2)}) collective-permute-start(f32[128,256]{0,1:T(8,128)S(1)} %maximum_add_fusion.5), channel_id=1, source_target_pairs={{0,1},{1,2},{2,3},{3,4},{4,5},{5,6},{6,7},{7,8},{8,9},{9,10},{10,1... | collective-permute-start | bytes 393224 | tf_op jit(solution)/shard_map/while/body/eval_jaxpr/ppermute | solution.py:13
  236.5 6.6 %collective-permute-start.2 = (f32[128,256]{0,1:T(8,128)S(1)}, f32[128,256]{0,1:T(8,128)S(1)}, u32[]{:S(2)}, u32[]{:S(2)}) collective-permute-start(f32[128,256]{0,1:T(8,128)S(1)} %maximum_add_fusion.4), channel_id=1, source_target_pairs={{0,1},{1,2},{2,3},{3,4},{4,5},{5,6},{6,7},{7,8},{8,9},{9,10},{10,1... | collective-permute-start | bytes 393224 | tf_op jit(solution)/shard_map/while/body/eval_jaxpr/ppermute | solution.py:13
  243.1 6.6 %collective-permute-start.3 = (f32[128,256]{0,1:T(8,128)S(1)}, f32[128,256]{0,1:T(8,128)S(1)}, u32[]{:S(2)}, u32[]{:S(2)}) collective-permute-start(f32[128,256]{0,1:T(8,128)S(1)} %maximum_add_fusion.5), channel_id=1, source_target_pairs={{0,1},{1,2},{2,3},{3,4},{4,5},{5,6},{6,7},{7,8},{8,9},{9,10},{10,1... | collective-permute-start | bytes 393224 | tf_op jit(solution)/shard_map/while/body/eval_jaxpr/ppermute | solution.py:13
  252.1 6.6 %collective-permute-start.2 = (f32[128,256]{0,1:T(8,128)S(1)}, f32[128,256]{0,1:T(8,128)S(1)}, u32[]{:S(2)}, u32[]{:S(2)}) collective-permute-start(f32[128,256]{0,1:T(8,128)S(1)} %maximum_add_fusion.4), channel_id=1, source_target_pairs={{0,1},{1,2},{2,3},{3,4},{4,5},{5,6},{6,7},{7,8},{8,9},{9,10},{10,1... | collective-permute-start | bytes 393224 | tf_op jit(solution)/shard_map/while/body/eval_jaxpr/ppermute | solution.py:13
  258.7 6.6 %collective-permute-start.3 = (f32[128,256]{0,1:T(8,128)S(1)}, f32[128,256]{0,1:T(8,128)S(1)}, u32[]{:S(2)}, u32[]{:S(2)}) collective-permute-start(f32[128,256]{0,1:T(8,128)S(1)} %maximum_add_fusion.5), channel_id=1, source_target_pairs={{0,1},{1,2},{2,3},{3,4},{4,5},{5,6},{6,7},{7,8},{8,9},{9,10},{10,1... | collective-permute-start | bytes 393224 | tf_op jit(solution)/shard_map/while/body/eval_jaxpr/ppermute | solution.py:13
  267.7 6.6 %collective-permute-start.2 = (f32[128,256]{0,1:T(8,128)S(1)}, f32[128,256]{0,1:T(8,128)S(1)}, u32[]{:S(2)}, u32[]{:S(2)}) collective-permute-start(f32[128,256]{0,1:T(8,128)S(1)} %maximum_add_fusion.4), channel_id=1, source_target_pairs={{0,1},{1,2},{2,3},{3,4},{4,5},{5,6},{6,7},{7,8},{8,9},{9,10},{10,1... | collective-permute-start | bytes 393224 | tf_op jit(solution)/shard_map/while/body/eval_jaxpr/ppermute | solution.py:13
  274.3 6.6 %collective-permute-start.3 = (f32[128,256]{0,1:T(8,128)S(1)}, f32[128,256]{0,1:T(8,128)S(1)}, u32[]{:S(2)}, u32[]{:S(2)}) collective-permute-start(f32[128,256]{0,1:T(8,128)S(1)} %maximum_add_fusion.5), channel_id=1, source_target_pairs={{0,1},{1,2},{2,3},{3,4},{4,5},{5,6},{6,7},{7,8},{8,9},{9,10},{10,1... | collective-permute-start | bytes 393224 | tf_op jit(solution)/shard_map/while/body/eval_jaxpr/ppermute | solution.py:13
  289.9 6.6 %collective-permute-start.3 = (f32[128,256]{0,1:T(8,128)S(1)}, f32[128,256]{0,1:T(8,128)S(1)}, u32[]{:S(2)}, u32[]{:S(2)}) collective-permute-start(f32[128,256]{0,1:T(8,128)S(1)} %maximum_add_fusion.5), channel_id=1, source_target_pairs={{0,1},{1,2},{2,3},{3,4},{4,5},{5,6},{6,7},{7,8},{8,9},{9,10},{10,1... | collective-permute-start | bytes 393224 | tf_op jit(solution)/shard_map/while/body/eval_jaxpr/ppermute | solution.py:13
  299.0 6.6 %collective-permute-start.2 = (f32[128,256]{0,1:T(8,128)S(1)}, f32[128,256]{0,1:T(8,128)S(1)}, u32[]{:S(2)}, u32[]{:S(2)}) collective-permute-start(f32[128,256]{0,1:T(8,128)S(1)} %maximum_add_fusion.4), channel_id=1, source_target_pairs={{0,1},{1,2},{2,3},{3,4},{4,5},{5,6},{6,7},{7,8},{8,9},{9,10},{10,1... | collective-permute-start | bytes 393224 | tf_op jit(solution)/shard_map/while/body/eval_jaxpr/ppermute | solution.py:13
  305.6 6.6 %collective-permute-start.3 = (f32[128,256]{0,1:T(8,128)S(1)}, f32[128,256]{0,1:T(8,128)S(1)}, u32[]{:S(2)}, u32[]{:S(2)}) collective-permute-start(f32[128,256]{0,1:T(8,128)S(1)} %maximum_add_fusion.5), channel_id=1, source_target_pairs={{0,1},{1,2},{2,3},{3,4},{4,5},{5,6},{6,7},{7,8},{8,9},{9,10},{10,1... | collective-permute-start | bytes 393224 | tf_op jit(solution)/shard_map/while/body/eval_jaxpr/ppermute | solution.py:13
  321.2 6.6 %collective-permute-start.3 = (f32[128,256]{0,1:T(8,128)S(1)}, f32[128,256]{0,1:T(8,128)S(1)}, u32[]{:S(2)}, u32[]{:S(2)}) collective-permute-start(f32[128,256]{0,1:T(8,128)S(1)} %maximum_add_fusion.5), channel_id=1, source_target_pairs={{0,1},{1,2},{2,3},{3,4},{4,5},{5,6},{6,7},{7,8},{8,9},{9,10},{10,1... | collective-permute-start | bytes 393224 | tf_op jit(solution)/shard_map/while/body/eval_jaxpr/ppermute | solution.py:13
  336.8 6.6 %collective-permute-start.3 = (f32[128,256]{0,1:T(8,128)S(1)}, f32[128,256]{0,1:T(8,128)S(1)}, u32[]{:S(2)}, u32[]{:S(2)}) collective-permute-start(f32[128,256]{0,1:T(8,128)S(1)} %maximum_add_fusion.5), channel_id=1, source_target_pairs={{0,1},{1,2},{2,3},{3,4},{4,5},{5,6},{6,7},{7,8},{8,9},{9,10},{10,1... | collective-permute-start | bytes 393224 | tf_op jit(solution)/shard_map/while/body/eval_jaxpr/ppermute | solution.py:13
  352.4 6.6 %collective-permute-start.3 = (f32[128,256]{0,1:T(8,128)S(1)}, f32[128,256]{0,1:T(8,128)S(1)}, u32[]{:S(2)}, u32[]{:S(2)}) collective-permute-start(f32[128,256]{0,1:T(8,128)S(1)} %maximum_add_fusion.5), channel_id=1, source_target_pairs={{0,1},{1,2},{2,3},{3,4},{4,5},{5,6},{6,7},{7,8},{8,9},{9,10},{10,1... | collective-permute-start | bytes 393224 | tf_op jit(solution)/shard_map/while/body/eval_jaxpr/ppermute | solution.py:13
  368.0 6.6 %collective-permute-start.3 = (f32[128,256]{0,1:T(8,128)S(1)}, f32[128,256]{0,1:T(8,128)S(1)}, u32[]{:S(2)}, u32[]{:S(2)}) collective-permute-start(f32[128,256]{0,1:T(8,128)S(1)} %maximum_add_fusion.5), channel_id=1, source_target_pairs={{0,1},{1,2},{2,3},{3,4},{4,5},{5,6},{6,7},{7,8},{8,9},{9,10},{10,1... | collective-permute-start | bytes 393224 | tf_op jit(solution)/shard_map/while/body/eval_jaxpr/ppermute | solution.py:13
  377.4 214.4 %all-reduce.2.cloned.1.call-start = ((), (), s32[]{:S(2)}) async-start(), calls=%async_computation.2 | async-start | bytes 262144 | tf_op jit(solution)/shard_map/psum | solution.py:136
  (119 other events, 955.2 us)
Sparse Core Ops, SparseCore 0:
  10.4 66.4 all-gather.2
  377.6 122.8 reduce-scatter.1
  503.1 88.6 all-reduce.1
where the time goes:
time: 601 us; the launch traced here: 600 us
  waiting for transfers between devices  433 us (72%)
  matrix products  82.5 us (14%)
  local copies, waits for them, and re-layouts  28.8 us (5%)
  other arithmetic  23.3 us (4%)
  between operations  13.9 us (2%)
  starting transfers between devices  10.3 us (2%)
  loops' own time  8.65 us (1%)
    ppermute x64, waiting for transfers between devices, from_behind(): lax.ppermute(x, axis, [(i, (i + by) % length) for i in range(length)])  155 us
    reduce_scatter x1, waiting for transfers between devices, on_device(): lax.psum_scatter(contract_rows(x_local, kv_grad_low), 'ctx', scatter_dime...  123 us
    psum x1, waiting for transfers between devices, on_device(): weight_total = lax.psum(weight_shard, 'dp')  90.5 us
    all_gather x1, waiting for transfers between devices, on_device(): kv_piece = lax.all_gather(kv_local, 'ctx', axis=0, tiled=True)  64.4 us
    dot_general x32, matrix products, backward_block(): jnp.dot(q_rows, kv_block[:, :HD].T, preferred_element_type=jnp.float32)  24.5 us
    dot_general x65, matrix products, contract_rows(): lax.dot_general(left_side, right_side, (((0,), (0,)), ((), ())), preferre...  20.6 us
    dot_general x32, matrix products, backward_block(): jnp.dot(low_score, kv_block[:, :HD], preferred_element_type=jnp.float32)  19.4 us
    reduce_sum x8, other arithmetic, forward_block(): new_sum = running_sum * factor + jnp.sum(expo_terms, axis=1)  13.4 us
  transfers between devices with their start and end apart: 67, of which 65 were waited for; matrix products, arithmetic and copies ran while one was open for 13% of the time, Pallas kernels for 0%

commit v1 on v0

--- a/solution.py
+++ b/solution.py
@@ -133,7 +133,8 @@
     weight_shard = lax.psum_scatter(
         contract_rows(x_local, kv_grad_low), "ctx", scatter_dimension=0, tiled=True
     )
-    weight_total = lax.psum(weight_shard, "dp")
+    parts = lax.all_gather(weight_shard, "dp")
+    weight_total = jnp.sum(parts, axis=0)
     return (grad_q_out, kv_grad_low.reshape(1, 1, local_count, 2 * HD), weight_total / dp_count)
 
 

time: 601 us -> 564 us (0.938)
  waiting for transfers between devices: 433 us -> 394 us
    psum x1 -> x0, waiting for transfers between devices: 90.5 us -> none  [on_device(): weight_total = lax.psum(weight_shard, 'dp')]
    all_gather x0 -> x1, waiting for transfers between devices: none -> 51.9 us  [on_device(): parts = lax.all_gather(weight_shard, 'dp')]
  transfers between devices with their start and end apart: 67 -> 67, of which waited for: 65 -> 65; matrix products, arithmetic and copies ran while one was open for 13% -> 14% of each run, Pallas kernels for 0% -> 0%
where the time goes in v1:
time: 564 us; the launch traced here: 562 us
  waiting for transfers between devices  394 us (70%)
  matrix products  82.5 us (15%)
  local copies, waits for them, and re-layouts  30.2 us (5%)
  other arithmetic  22.7 us (4%)
  between operations  13.9 us (2%)
  starting transfers between devices  10.4 us (2%)
  loops' own time  8.67 us (2%)
    ppermute x64, waiting for transfers between devices, from_behind(): lax.ppermute(x, axis, [(i, (i + by) % length) for i in range(length)])  154 us
    reduce_scatter x1, waiting for transfers between devices, on_device(): lax.psum_scatter(contract_rows(x_local, kv_grad_low), 'ctx', scatter_dime...  123 us
    all_gather x1, waiting for transfers between devices, on_device(): kv_piece = lax.all_gather(kv_local, 'ctx', axis=0, tiled=True)  64.4 us
    all_gather x1, waiting for transfers between devices, on_device(): parts = lax.all_gather(weight_shard, 'dp')  51.9 us
    dot_general x32, matrix products, backward_block(): jnp.dot(q_rows, kv_block[:, :HD].T, preferred_element_type=jnp.float32)  24.5 us
    dot_general x65, matrix products, contract_rows(): lax.dot_general(left_side, right_side, (((0,), (0,)), ((), ())), preferre...  20.5 us
    dot_general x32, matrix products, backward_block(): jnp.dot(low_score, kv_block[:, :HD], preferred_element_type=jnp.float32)  19.4 us
    reduce_sum x8, other arithmetic, forward_block(): new_sum = running_sum * factor + jnp.sum(expo_terms, axis=1)  13.4 us
  transfers between devices with their start and end apart: 67, of which 65 were waited for; matrix products, arithmetic and copies ran while one was open for 14% of the time, Pallas kernels for 0%

profile of v1, /device:TPU:32, one launch (start us, length us, event | category | flops | bytes accessed | tf_op | source)
XLA Modules:
  0.0 562.2 jit_solution(16175852171753326342)
XLA Ops:
  12.6 64.4 %all-gather.5.cloned.1.call-done = bf16[1,1,4096,256]{3,2,1,0:T(8,128)(2,1)} async-done(((bf16[1,1,128,256]{3,2,1,0:T(8,128)(2,1)}), bf16[1,1,4096,256]{3,2,1,0:T(8,128)(2,1)}) %all-gather.5.cloned.1.call-update) | async-done | bytes 2097168 | tf_op jit(solution)/shard_map/all_gather | solution.py:81
  77.0 55.6 %while.41 = (s32[]{:T(128)}, f32[1024]{0:T(1024)S(1)}, f32[1024]{0:T(1024)S(1)}, f32[1024]{0:T(1024)S(1)}, s32[8]{0:T(128)S(1)}, /*index=5*/s32[10]{0:T(128)S(1)...) while((s32[]{:T(128)}, f32[1024]{0:T(1024)S(1)}, ...), condition=%wide.region_7.8_spmd.clone, body=%wide.region_1.7_spmd.clone.sunk | while | flops 275166080 | bytes 18316680 | solution.py:89
  132.6 241.9 %while.42 = (s32[]{:T(128)}, f32[1024,128]{1,0:T(8,128)}, bf16[128,256]{1,0:T(8,128)(2,1)S(1)}, f32[128,256]{0,1:T(8,128)S(1)}, s32[]{:T(128)}, /*index=5*/s32[1...) while((s32[]{:T(128)}, f32[1024,128]{1,0:T(8,128)}, ...), condition=%wide.region_12.13_spmd.clone.clone.clone, body=%wide.region_8.12_spmd.clone.clone.clone.sunk | while | flops 338411936 | bytes 14973101 | solution.py:129
  166.2 3.0 collective-permute-done.1
  174.4 3.1 collective-permute-done
  181.8 3.0 collective-permute-done.1
  190.0 3.1 collective-permute-done
  197.4 3.0 collective-permute-done.1
  205.6 3.1 collective-permute-done
  213.0 3.0 collective-permute-done.1
  221.2 3.1 collective-permute-done
  236.8 3.1 collective-permute-done
  252.4 3.1 collective-permute-done
  268.0 3.1 collective-permute-done
  283.6 3.1 collective-permute-done
  299.2 3.1 collective-permute-done
  314.8 3.1 collective-permute-done
  322.2 3.0 collective-permute-done.1
  330.4 3.1 collective-permute-done
  346.0 3.1 collective-permute-done
  353.4 3.0 collective-permute-done.1
  361.6 3.1 collective-permute-done
  377.4 123.0 %reduce-scatter.2.cloned.1.call-done = f32[128,256]{0,1:T(8,128)} async-done(((f32[4096,256]{0,1:T(8,128)}), f32[128,256]{0,1:T(8,128)}) %reduce-scatter.2.cloned.1.call-update) | async-done | bytes 131088 | tf_op jit(solution)/shard_map/reduce_scatter | solution.py:133
  501.3 51.9 %all-gather.7.cloned.1.call-done = f32[1024,256]{0,1:T(8,128)} async-done(((f32[128,256]{0,1:T(8,128)}), f32[1024,256]{0,1:T(8,128)}) %all-gather.7.cloned.1.call-update) | async-done | bytes 1048592 | tf_op jit(solution)/shard_map/all_gather | solution.py:136
  (750 shorter events, 242.6 us)
Async XLA Ops:
  7.2 69.8 %all-gather.5.cloned.1.call-start = ((), (), s32[]{:S(2)}) async-start(), calls=%async_computation.2 | async-start | bytes 2162688 | tf_op jit(solution)/shard_map/all_gather | solution.py:81
  8.8 491.6 %reduce-scatter.2.cloned.1.call-start = ((), (), s32[]{:S(2)}) async-start(), calls=%async_computation.1 | async-start | bytes 4325376 | tf_op jit(solution)/shard_map/reduce_scatter | solution.py:133
  158.5 6.6 %collective-permute-start.2 = (f32[128,256]{0,1:T(8,128)S(1)}, f32[128,256]{0,1:T(8,128)S(1)}, u32[]{:S(2)}, u32[]{:S(2)}) collective-permute-start(f32[128,256]{0,1:T(8,128)S(1)} %maximum_add_fusion.4), channel_id=1, source_target_pairs={{0,1},{1,2},{2,3},{3,4},{4,5},{5,6},{6,7},{7,8},{8,9},{9,10},{10,1... | collective-permute-start | bytes 393224 | tf_op jit(solution)/shard_map/while/body/eval_jaxpr/ppermute | solution.py:13
  174.1 6.6 %collective-permute-start.2 = (f32[128,256]{0,1:T(8,128)S(1)}, f32[128,256]{0,1:T(8,128)S(1)}, u32[]{:S(2)}, u32[]{:S(2)}) collective-permute-start(f32[128,256]{0,1:T(8,128)S(1)} %maximum_add_fusion.4), channel_id=1, source_target_pairs={{0,1},{1,2},{2,3},{3,4},{4,5},{5,6},{6,7},{7,8},{8,9},{9,10},{10,1... | collective-permute-start | bytes 393224 | tf_op jit(solution)/shard_map/while/body/eval_jaxpr/ppermute | solution.py:13
  180.7 6.6 %collective-permute-start.3 = (f32[128,256]{0,1:T(8,128)S(1)}, f32[128,256]{0,1:T(8,128)S(1)}, u32[]{:S(2)}, u32[]{:S(2)}) collective-permute-start(f32[128,256]{0,1:T(8,128)S(1)} %maximum_add_fusion.5), channel_id=1, source_target_pairs={{0,1},{1,2},{2,3},{3,4},{4,5},{5,6},{6,7},{7,8},{8,9},{9,10},{10,1... | collective-permute-start | bytes 393224 | tf_op jit(solution)/shard_map/while/body/eval_jaxpr/ppermute | solution.py:13
  189.7 6.6 %collective-permute-start.2 = (f32[128,256]{0,1:T(8,128)S(1)}, f32[128,256]{0,1:T(8,128)S(1)}, u32[]{:S(2)}, u32[]{:S(2)}) collective-permute-start(f32[128,256]{0,1:T(8,128)S(1)} %maximum_add_fusion.4), channel_id=1, source_target_pairs={{0,1},{1,2},{2,3},{3,4},{4,5},{5,6},{6,7},{7,8},{8,9},{9,10},{10,1... | collective-permute-start | bytes 393224 | tf_op jit(solution)/shard_map/while/body/eval_jaxpr/ppermute | solution.py:13
  205.3 6.6 %collective-permute-start.2 = (f32[128,256]{0,1:T(8,128)S(1)}, f32[128,256]{0,1:T(8,128)S(1)}, u32[]{:S(2)}, u32[]{:S(2)}) collective-permute-start(f32[128,256]{0,1:T(8,128)S(1)} %maximum_add_fusion.4), channel_id=1, source_target_pairs={{0,1},{1,2},{2,3},{3,4},{4,5},{5,6},{6,7},{7,8},{8,9},{9,10},{10,1... | collective-permute-start | bytes 393224 | tf_op jit(solution)/shard_map/while/body/eval_jaxpr/ppermute | solution.py:13
  211.9 6.6 %collective-permute-start.3 = (f32[128,256]{0,1:T(8,128)S(1)}, f32[128,256]{0,1:T(8,128)S(1)}, u32[]{:S(2)}, u32[]{:S(2)}) collective-permute-start(f32[128,256]{0,1:T(8,128)S(1)} %maximum_add_fusion.5), channel_id=1, source_target_pairs={{0,1},{1,2},{2,3},{3,4},{4,5},{5,6},{6,7},{7,8},{8,9},{9,10},{10,1... | collective-permute-start | bytes 393224 | tf_op jit(solution)/shard_map/while/body/eval_jaxpr/ppermute | solution.py:13
  220.9 6.6 %collective-permute-start.2 = (f32[128,256]{0,1:T(8,128)S(1)}, f32[128,256]{0,1:T(8,128)S(1)}, u32[]{:S(2)}, u32[]{:S(2)}) collective-permute-start(f32[128,256]{0,1:T(8,128)S(1)} %maximum_add_fusion.4), channel_id=1, source_target_pairs={{0,1},{1,2},{2,3},{3,4},{4,5},{5,6},{6,7},{7,8},{8,9},{9,10},{10,1... | collective-permute-start | bytes 393224 | tf_op jit(solution)/shard_map/while/body/eval_jaxpr/ppermute | solution.py:13
  236.5 6.6 %collective-permute-start.2 = (f32[128,256]{0,1:T(8,128)S(1)}, f32[128,256]{0,1:T(8,128)S(1)}, u32[]{:S(2)}, u32[]{:S(2)}) collective-permute-start(f32[128,256]{0,1:T(8,128)S(1)} %maximum_add_fusion.4), channel_id=1, source_target_pairs={{0,1},{1,2},{2,3},{3,4},{4,5},{5,6},{6,7},{7,8},{8,9},{9,10},{10,1... | collective-permute-start | bytes 393224 | tf_op jit(solution)/shard_map/while/body/eval_jaxpr/ppermute | solution.py:13
  243.1 6.6 %collective-permute-start.3 = (f32[128,256]{0,1:T(8,128)S(1)}, f32[128,256]{0,1:T(8,128)S(1)}, u32[]{:S(2)}, u32[]{:S(2)}) collective-permute-start(f32[128,256]{0,1:T(8,128)S(1)} %maximum_add_fusion.5), channel_id=1, source_target_pairs={{0,1},{1,2},{2,3},{3,4},{4,5},{5,6},{6,7},{7,8},{8,9},{9,10},{10,1... | collective-permute-start | bytes 393224 | tf_op jit(solution)/shard_map/while/body/eval_jaxpr/ppermute | solution.py:13
  252.1 6.6 %collective-permute-start.2 = (f32[128,256]{0,1:T(8,128)S(1)}, f32[128,256]{0,1:T(8,128)S(1)}, u32[]{:S(2)}, u32[]{:S(2)}) collective-permute-start(f32[128,256]{0,1:T(8,128)S(1)} %maximum_add_fusion.4), channel_id=1, source_target_pairs={{0,1},{1,2},{2,3},{3,4},{4,5},{5,6},{6,7},{7,8},{8,9},{9,10},{10,1... | collective-permute-start | bytes 393224 | tf_op jit(solution)/shard_map/while/body/eval_jaxpr/ppermute | solution.py:13
  258.7 6.6 %collective-permute-start.3 = (f32[128,256]{0,1:T(8,128)S(1)}, f32[128,256]{0,1:T(8,128)S(1)}, u32[]{:S(2)}, u32[]{:S(2)}) collective-permute-start(f32[128,256]{0,1:T(8,128)S(1)} %maximum_add_fusion.5), channel_id=1, source_target_pairs={{0,1},{1,2},{2,3},{3,4},{4,5},{5,6},{6,7},{7,8},{8,9},{9,10},{10,1... | collective-permute-start | bytes 393224 | tf_op jit(solution)/shard_map/while/body/eval_jaxpr/ppermute | solution.py:13
  267.7 6.6 %collective-permute-start.2 = (f32[128,256]{0,1:T(8,128)S(1)}, f32[128,256]{0,1:T(8,128)S(1)}, u32[]{:S(2)}, u32[]{:S(2)}) collective-permute-start(f32[128,256]{0,1:T(8,128)S(1)} %maximum_add_fusion.4), channel_id=1, source_target_pairs={{0,1},{1,2},{2,3},{3,4},{4,5},{5,6},{6,7},{7,8},{8,9},{9,10},{10,1... | collective-permute-start | bytes 393224 | tf_op jit(solution)/shard_map/while/body/eval_jaxpr/ppermute | solution.py:13
  274.3 6.6 %collective-permute-start.3 = (f32[128,256]{0,1:T(8,128)S(1)}, f32[128,256]{0,1:T(8,128)S(1)}, u32[]{:S(2)}, u32[]{:S(2)}) collective-permute-start(f32[128,256]{0,1:T(8,128)S(1)} %maximum_add_fusion.5), channel_id=1, source_target_pairs={{0,1},{1,2},{2,3},{3,4},{4,5},{5,6},{6,7},{7,8},{8,9},{9,10},{10,1... | collective-permute-start | bytes 393224 | tf_op jit(solution)/shard_map/while/body/eval_jaxpr/ppermute | solution.py:13
  283.3 6.6 %collective-permute-start.2 = (f32[128,256]{0,1:T(8,128)S(1)}, f32[128,256]{0,1:T(8,128)S(1)}, u32[]{:S(2)}, u32[]{:S(2)}) collective-permute-start(f32[128,256]{0,1:T(8,128)S(1)} %maximum_add_fusion.4), channel_id=1, source_target_pairs={{0,1},{1,2},{2,3},{3,4},{4,5},{5,6},{6,7},{7,8},{8,9},{9,10},{10,1... | collective-permute-start | bytes 393224 | tf_op jit(solution)/shard_map/while/body/eval_jaxpr/ppermute | solution.py:13
  289.9 6.6 %collective-permute-start.3 = (f32[128,256]{0,1:T(8,128)S(1)}, f32[128,256]{0,1:T(8,128)S(1)}, u32[]{:S(2)}, u32[]{:S(2)}) collective-permute-start(f32[128,256]{0,1:T(8,128)S(1)} %maximum_add_fusion.5), channel_id=1, source_target_pairs={{0,1},{1,2},{2,3},{3,4},{4,5},{5,6},{6,7},{7,8},{8,9},{9,10},{10,1... | collective-permute-start | bytes 393224 | tf_op jit(solution)/shard_map/while/body/eval_jaxpr/ppermute | solution.py:13
  298.9 6.6 %collective-permute-start.2 = (f32[128,256]{0,1:T(8,128)S(1)}, f32[128,256]{0,1:T(8,128)S(1)}, u32[]{:S(2)}, u32[]{:S(2)}) collective-permute-start(f32[128,256]{0,1:T(8,128)S(1)} %maximum_add_fusion.4), channel_id=1, source_target_pairs={{0,1},{1,2},{2,3},{3,4},{4,5},{5,6},{6,7},{7,8},{8,9},{9,10},{10,1... | collective-permute-start | bytes 393224 | tf_op jit(solution)/shard_map/while/body/eval_jaxpr/ppermute | solution.py:13
  305.5 6.6 %collective-permute-start.3 = (f32[128,256]{0,1:T(8,128)S(1)}, f32[128,256]{0,1:T(8,128)S(1)}, u32[]{:S(2)}, u32[]{:S(2)}) collective-permute-start(f32[128,256]{0,1:T(8,128)S(1)} %maximum_add_fusion.5), channel_id=1, source_target_pairs={{0,1},{1,2},{2,3},{3,4},{4,5},{5,6},{6,7},{7,8},{8,9},{9,10},{10,1... | collective-permute-start | bytes 393224 | tf_op jit(solution)/shard_map/while/body/eval_jaxpr/ppermute | solution.py:13
  314.5 6.6 %collective-permute-start.2 = (f32[128,256]{0,1:T(8,128)S(1)}, f32[128,256]{0,1:T(8,128)S(1)}, u32[]{:S(2)}, u32[]{:S(2)}) collective-permute-start(f32[128,256]{0,1:T(8,128)S(1)} %maximum_add_fusion.4), channel_id=1, source_target_pairs={{0,1},{1,2},{2,3},{3,4},{4,5},{5,6},{6,7},{7,8},{8,9},{9,10},{10,1... | collective-permute-start | bytes 393224 | tf_op jit(solution)/shard_map/while/body/eval_jaxpr/ppermute | solution.py:13
  330.1 6.6 %collective-permute-start.2 = (f32[128,256]{0,1:T(8,128)S(1)}, f32[128,256]{0,1:T(8,128)S(1)}, u32[]{:S(2)}, u32[]{:S(2)}) collective-permute-start(f32[128,256]{0,1:T(8,128)S(1)} %maximum_add_fusion.4), channel_id=1, source_target_pairs={{0,1},{1,2},{2,3},{3,4},{4,5},{5,6},{6,7},{7,8},{8,9},{9,10},{10,1... | collective-permute-start | bytes 393224 | tf_op jit(solution)/shard_map/while/body/eval_jaxpr/ppermute | solution.py:13
  345.7 6.6 %collective-permute-start.2 = (f32[128,256]{0,1:T(8,128)S(1)}, f32[128,256]{0,1:T(8,128)S(1)}, u32[]{:S(2)}, u32[]{:S(2)}) collective-permute-start(f32[128,256]{0,1:T(8,128)S(1)} %maximum_add_fusion.4), channel_id=1, source_target_pairs={{0,1},{1,2},{2,3},{3,4},{4,5},{5,6},{6,7},{7,8},{8,9},{9,10},{10,1... | collective-permute-start | bytes 393224 | tf_op jit(solution)/shard_map/while/body/eval_jaxpr/ppermute | solution.py:13
  361.3 6.6 %collective-permute-start.2 = (f32[128,256]{0,1:T(8,128)S(1)}, f32[128,256]{0,1:T(8,128)S(1)}, u32[]{:S(2)}, u32[]{:S(2)}) collective-permute-start(f32[128,256]{0,1:T(8,128)S(1)} %maximum_add_fusion.4), channel_id=1, source_target_pairs={{0,1},{1,2},{2,3},{3,4},{4,5},{5,6},{6,7},{7,8},{8,9},{9,10},{10,1... | collective-permute-start | bytes 393224 | tf_op jit(solution)/shard_map/while/body/eval_jaxpr/ppermute | solution.py:13
  377.3 175.8 %all-gather.7.cloned.1.call-start = ((), (), s32[]{:S(2)}) async-start(), calls=%async_computation.3 | async-start | bytes 1179648 | tf_op jit(solution)/shard_map/all_gather | solution.py:136
  (119 other events, 954.9 us)
Sparse Core Ops, SparseCore 0:
  10.4 66.4 all-gather.4
  377.4 122.9 reduce-scatter.1
  502.9 50.2 all-gather.6
